TPU v7x, 32 devices: a whole 2x2x4 slice. The times are simulated.
32 devices in a mesh: dp: 16 (over z, y, core), seq: 2 (over x).
Axes of the slice: x: 2, y: 2, z: 4, core: 2. Of those that a mesh axis runs over, the one named last changes fastest.
Arguments:
- latents: bfloat16 [2, 16, 1024, 1152], P(None, 'dp', 'seq'), may hold values from -6 to 6
- cond: float32 [24, 1152], replicated, may hold values from -6 to 6
- slot_mask: int32 [2, 16], replicated, may hold values from 0 to 1, as said below
- slot_image: int32 [2, 16], replicated, may hold values from 0 to 23, as said below
- teacher: bfloat16 [2, 16, 1024, 1152], P(None, 'dp', 'seq'), may hold values from -6 to 6
- cotangent: bfloat16 [2, 16, 1024, 1152], P(None, 'dp', 'seq'), may hold values from -6 to 6
- ada_w: bfloat16 [1152, 6912], P('dp', 'seq'), may hold values from -0.1875 to 0.1875
- ada_b: float32 [6912], replicated, may hold values from -3 to 3
- qkv_w: bfloat16 [1152, 3456], P('dp', 'seq'), may hold values from -0.1875 to 0.1875
- qv_b: float32 [2304], replicated, may hold values from -2 to 2
- proj_w: bfloat16 [1152, 1152], P('dp', 'seq'), may hold values from -1.5 to 1.5
- proj_b: float32 [1152], replicated, may hold values from -2 to 2
- fc1_w: bfloat16 [1152, 4608], P('dp', 'seq'), may hold values from -0.1875 to 0.1875
- fc1_b: float32 [4608], replicated, may hold values from -2 to 2
- fc2_w: bfloat16 [4608, 1152], P('dp', 'seq'), may hold values from -0.09375 to 0.09375
- fc2_b: float32 [1152], replicated, may hold values from -2 to 2
Outputs:
- block_out: bfloat16 [2, 16, 1024, 1152], P(None, 'dp', 'seq')
- latents_grad: float32 [2, 16, 1024, 1152], P(None, 'dp', 'seq')
- loss: float32 [], replicated
- cond_grad: float32 [24, 1152], replicated
- ada_w_grad: float32 [1152, 6912], P('dp', 'seq')
- ada_b_grad: float32 [6912], replicated
- qkv_w_grad: float32 [1152, 3456], P('dp', 'seq')
- qv_b_grad: float32 [2304], replicated
- proj_w_grad: float32 [1152, 1152], P('dp', 'seq')
- proj_b_grad: float32 [1152], replicated
- fc1_w_grad: float32 [1152, 4608], P('dp', 'seq')
- fc1_b_grad: float32 [4608], replicated
- fc2_w_grad: float32 [4608, 1152], P('dp', 'seq')
- fc2_b_grad: float32 [1152], replicated
Inputs may be any that keep to these rules, and one draw needn't show every extreme that they name: Micro-batch i holds the images n with n mod 2 = i, each in exactly one slot with slot_mask 1; all other slots have slot_mask 0. `slot_image`: in a slot with slot_mask 1, the image it holds; in a pad slot any image number.
All inputs are finite; a program needn't handle non-finite values.
Results may differ from a plain program's by a relative error of at most 0.018.
The roundings to bfloat16 on the way count: a program that leaves them out, or rounds other values in their place, can miss the bound.
Values may be sent and summed in bfloat16 or wider, within the bound.
A program may use at most 448 MiB of HBM per device.

v0:
```python
import jax
import jax.numpy as jnp
from jax import lax
from jax.sharding import PartitionSpec as P

HEADS = 16
HIGH = lax.Precision.HIGHEST


def layer_norm(value):
    center = value - jnp.mean(value, axis=-1, keepdims=True)
    spread = jnp.mean(center * center, axis=-1, keepdims=True)
    return center * lax.rsqrt(spread + 1e-06)


def gelu_tanh(value):
    return jax.nn.gelu(value, approximate=True)


def local(
    latents,
    cond,
    slot_mask,
    slot_image,
    teacher,
    cotangent,
    ada_w,
    ada_b,
    qkv_w,
    qv_b,
    proj_w,
    proj_b,
    fc1_w,
    fc1_b,
    fc2_w,
    fc2_b,
):
    f32 = jnp.float32
    bf16 = jnp.bfloat16
    micro = latents.shape[0]
    slots_dev = latents.shape[1]
    local_len = latents.shape[2]
    width = latents.shape[3]
    images = cond.shape[0]
    heads = HEADS
    head_size = width // heads
    full_len = local_len * lax.axis_size("seq")
    hidden_units = fc1_b.shape[0]
    scale = head_size ** (-0.5)
    dp_index = lax.axis_index("dp")
    seq_index = lax.axis_index("seq")
    mod_cols = ada_w.shape[1]
    col_start = seq_index * mod_cols
    count = jnp.sum(slot_mask).astype(f32) * full_len
    divisor = count * width
    image_table = jnp.arange(images, dtype=jnp.int32)
    grad_qkv = jnp.zeros((width, 3 * width), f32)
    grad_proj = jnp.zeros((width, width), f32)
    grad_fc1 = jnp.zeros((width, hidden_units), f32)
    grad_fc2 = jnp.zeros((hidden_units, width), f32)
    grad_ada = jnp.zeros((width, mod_cols), f32)
    grad_cond = jnp.zeros((images, width), f32)
    bias_ada = jnp.zeros((6 * width,), f32)
    bias_qv = jnp.zeros((2 * width,), f32)
    bias_proj = jnp.zeros((width,), f32)
    bias_fc1 = jnp.zeros((hidden_units,), f32)
    bias_fc2 = jnp.zeros((width,), f32)
    loss_sum = jnp.zeros((), f32)
    column_ids = jnp.arange(6 * width, dtype=jnp.int32)
    in_mine = (column_ids >= col_start) & (column_ids < col_start + mod_cols)
    results = []
    input_grads = []
    for micro_index in range(micro):
        qkv_cols = lax.all_gather(qkv_w, "seq", axis=1, tiled=True)
        proj_cols = lax.all_gather(proj_w, "seq", axis=1, tiled=True)
        fc1_cols = lax.all_gather(fc1_w, "seq", axis=1, tiled=True)
        fc2_cols = lax.all_gather(fc2_w, "seq", axis=1, tiled=True)
        qkv_full = lax.all_gather(qkv_cols, "dp", axis=0, tiled=True)
        proj_full = lax.all_gather(proj_cols, "dp", axis=0, tiled=True)
        fc1_full = lax.all_gather(fc1_cols, "dp", axis=0, tiled=True)
        fc2_full = lax.all_gather(fc2_cols, "dp", axis=0, tiled=True)
        ada_cols = lax.all_gather(ada_w, "seq", axis=1, tiled=True)
        ada_full = lax.all_gather(ada_cols, "dp", axis=0, tiled=True)
        qkv_full, proj_full, fc1_full, fc2_full, ada_full = (
            qkv_full,
            proj_full,
            fc1_full,
            fc2_full,
            ada_full,
        )
        image_mine = lax.dynamic_slice_in_dim(
            slot_image[micro_index], dp_index * slots_dev, slots_dev
        )
        mask_mine = lax.dynamic_slice_in_dim(
            slot_mask[micro_index], dp_index * slots_dev, slots_dev
        ).astype(f32)
        pick_mine = (image_mine[:, None] == image_table[None, :]).astype(f32)
        cond_mine = jnp.dot(pick_mine, cond, precision=HIGH)
        silu_mine = jax.nn.silu(cond_mine).astype(bf16)
        modulation = jnp.dot(silu_mine, ada_full, preferred_element_type=f32) + ada_b
        pieces = [
            modulation[:, index * width : (index + 1) * width][:, None, :] for index in range(6)
        ]
        shift1, scale1, gate1, shift2, scale2, gate2 = pieces
        inputs = latents[micro_index].astype(f32)
        normed1 = layer_norm(inputs)
        hidden = (normed1 * (1.0 + scale1) + shift1).astype(bf16)
        joint = jnp.einsum("btd,de->bte", hidden, qkv_full, preferred_element_type=f32)
        query = (joint[..., :width] + qv_b[:width]).astype(bf16)
        keys_local = joint[..., width : 2 * width].astype(bf16)
        values_local = (joint[..., 2 * width :] + qv_b[width:]).astype(bf16)
        keys_all, values_all = (
            lax.all_gather(keys_local, "seq", axis=1, tiled=True),
            lax.all_gather(values_local, "seq", axis=1, tiled=True),
        )
        query_heads = query.reshape(slots_dev, local_len, heads, head_size)
        key_heads = keys_all.reshape(slots_dev, full_len, heads, head_size)
        value_heads = values_all.reshape(slots_dev, full_len, heads, head_size)
        scores = (
            jnp.einsum("bqhe,bkhe->bhqk", query_heads, key_heads, preferred_element_type=f32)
            * scale
        )
        row_top = jnp.max(scores, axis=-1, keepdims=True)
        row_total = jnp.sum(jnp.exp(scores - row_top), axis=-1, keepdims=True)
        probs_low = (jnp.exp(scores - row_top) / row_total).astype(bf16)
        attended = jnp.einsum("bhqk,bkhe->bqhe", probs_low, value_heads, preferred_element_type=f32)
        attended = attended.reshape(slots_dev, local_len, width).astype(bf16)
        branch = jnp.einsum("btd,de->bte", attended, proj_full, preferred_element_type=f32) + proj_b
        middle = inputs + gate1 * branch
        normed2 = layer_norm(middle)
        hidden2 = (normed2 * (1.0 + scale2) + shift2).astype(bf16)
        before = jnp.einsum("btd,df->btf", hidden2, fc1_full, preferred_element_type=f32) + fc1_b
        active = gelu_tanh(before).astype(bf16)
        mlp_out = jnp.einsum("btf,fd->btd", active, fc2_full, preferred_element_type=f32) + fc2_b
        result = middle + gate2 * mlp_out
        results.append(result.astype(bf16))
        valid = mask_mine[:, None, None]
        diff = result - teacher[micro_index].astype(f32)
        loss_sum = loss_sum + jnp.sum(valid * diff * diff)
        grad_out = valid * (2.0 * diff / divisor + cotangent[micro_index].astype(f32))
        d_gate2 = jnp.sum(grad_out * mlp_out, axis=1)
        d_mlp = (grad_out * gate2).astype(bf16)
        grad_fc2 = grad_fc2 + jnp.einsum("btf,btd->fd", active, d_mlp, preferred_element_type=f32)
        bias_fc2 = bias_fc2 + jnp.sum(d_mlp.astype(f32), axis=(0, 1))
        d_active = jnp.einsum("btd,fd->btf", d_mlp, fc2_full, preferred_element_type=f32)
        d_before = jax.vjp(gelu_tanh, before)[1](d_active)[0].astype(bf16)
        grad_fc1 = grad_fc1 + jnp.einsum(
            "btd,btf->df", hidden2, d_before, preferred_element_type=f32
        )
        bias_fc1 = bias_fc1 + jnp.sum(d_before.astype(f32), axis=(0, 1))
        d_hidden2 = jnp.einsum("btf,df->btd", d_before, fc1_full, preferred_element_type=f32)
        d_scale2 = jnp.sum(d_hidden2 * normed2, axis=1)
        d_shift2 = jnp.sum(d_hidden2, axis=1)
        d_middle = grad_out + jax.vjp(layer_norm, middle)[1](d_hidden2 * (1.0 + scale2))[0]
        d_gate1 = jnp.sum(d_middle * branch, axis=1)
        d_branch = (d_middle * gate1).astype(bf16)
        grad_proj = grad_proj + jnp.einsum(
            "btd,bte->de", attended, d_branch, preferred_element_type=f32
        )
        bias_proj = bias_proj + jnp.sum(d_branch.astype(f32), axis=(0, 1))
        d_attended = jnp.einsum(
            "bte,de->btd", d_branch, proj_full, preferred_element_type=f32
        ).astype(bf16)
        d_attended = d_attended.reshape(slots_dev, local_len, heads, head_size)
        again_scores = (
            jnp.einsum("bqhe,bkhe->bhqk", query_heads, key_heads, preferred_element_type=f32)
            * scale
        )
        probs = jnp.exp(again_scores - row_top) / row_total
        d_probs = jnp.einsum("bqhe,bkhe->bhqk", d_attended, value_heads, preferred_element_type=f32)
        row_inner = jnp.sum(probs * d_probs, axis=-1, keepdims=True)
        d_scores = (probs * (d_probs - row_inner)).astype(bf16)
        d_query = (
            jnp.einsum("bhqk,bkhe->bqhe", d_scores, key_heads, preferred_element_type=f32) * scale
        )
        key_terms = (
            jnp.einsum("bhqk,bqhe->bkhe", d_scores, query_heads, preferred_element_type=f32) * scale
        )
        value_terms = jnp.einsum(
            "bhqk,bqhe->bkhe", probs_low, d_attended, preferred_element_type=f32
        )
        key_terms = key_terms.reshape(slots_dev, full_len, width)
        value_terms = value_terms.reshape(slots_dev, full_len, width)
        d_keys, d_values = (
            lax.psum_scatter(
                key_terms.astype(jnp.bfloat16), "seq", scatter_dimension=1, tiled=True
            ).astype(jnp.float32),
            lax.psum_scatter(
                value_terms.astype(jnp.bfloat16), "seq", scatter_dimension=1, tiled=True
            ).astype(jnp.float32),
        )
        d_query = d_query.reshape(slots_dev, local_len, width).astype(bf16)
        d_joint = jnp.concatenate([d_query, d_keys.astype(bf16), d_values.astype(bf16)], axis=-1)
        grad_qkv = grad_qkv + jnp.einsum("btd,bte->de", hidden, d_joint, preferred_element_type=f32)
        bias_qv = bias_qv + jnp.concatenate(
            [
                jnp.sum(d_joint[..., :width].astype(f32), axis=(0, 1)),
                jnp.sum(d_joint[..., 2 * width :].astype(f32), axis=(0, 1)),
            ]
        )
        d_hidden = jnp.einsum("bte,de->btd", d_joint, qkv_full, preferred_element_type=f32)
        d_scale1 = jnp.sum(d_hidden * normed1, axis=1)
        d_shift1 = jnp.sum(d_hidden, axis=1)
        d_inputs = d_middle + jax.vjp(layer_norm, inputs)[1](d_hidden * (1.0 + scale1))[0]
        input_grads.append(d_inputs)
        mod_partial = jnp.concatenate(
            [d_shift1, d_scale1, d_gate1, d_shift2, d_scale2, d_gate2], axis=-1
        )
        d_mod = lax.psum(mod_partial, "seq").astype(bf16)
        own_cols = lax.dynamic_slice_in_dim(d_mod, col_start, mod_cols, 1)
        bias_ada = bias_ada + jnp.where(in_mine, jnp.sum(d_mod.astype(f32), axis=0), 0.0)
        grad_ada = grad_ada + jnp.dot(silu_mine.T, own_cols, preferred_element_type=f32)
        ada_own = lax.dynamic_slice_in_dim(ada_full, col_start, mod_cols, 1)
        d_cond = jnp.einsum("bm,dm->bd", own_cols, ada_own, preferred_element_type=f32)
        d_cond = jax.vjp(jax.nn.silu, cond_mine)[1](d_cond)[0]
        grad_cond = grad_cond + jnp.dot(pick_mine.T, d_cond, precision=HIGH)
    ada_w_grad = lax.psum_scatter(
        grad_ada.astype(jnp.bfloat16), "dp", scatter_dimension=0, tiled=True
    ).astype(jnp.float32)
    rows_qkv, rows_proj, rows_fc1, rows_fc2 = (
        lax.psum_scatter(
            grad_qkv.astype(jnp.bfloat16), "dp", scatter_dimension=0, tiled=True
        ).astype(jnp.float32),
        lax.psum_scatter(
            grad_proj.astype(jnp.bfloat16), "dp", scatter_dimension=0, tiled=True
        ).astype(jnp.float32),
        lax.psum_scatter(
            grad_fc1.astype(jnp.bfloat16), "dp", scatter_dimension=0, tiled=True
        ).astype(jnp.float32),
        lax.psum_scatter(
            grad_fc2.astype(jnp.bfloat16), "dp", scatter_dimension=0, tiled=True
        ).astype(jnp.float32),
    )
    qkv_w_grad, proj_w_grad, fc1_w_grad, fc2_w_grad = (
        lax.psum_scatter(
            rows_qkv.astype(jnp.bfloat16), "seq", scatter_dimension=1, tiled=True
        ).astype(jnp.float32),
        lax.psum_scatter(
            rows_proj.astype(jnp.bfloat16), "seq", scatter_dimension=1, tiled=True
        ).astype(jnp.float32),
        lax.psum_scatter(
            rows_fc1.astype(jnp.bfloat16), "seq", scatter_dimension=1, tiled=True
        ).astype(jnp.float32),
        lax.psum_scatter(
            rows_fc2.astype(jnp.bfloat16), "seq", scatter_dimension=1, tiled=True
        ).astype(jnp.float32),
    )
    summed = lax.psum(
        (loss_sum, bias_ada, bias_qv, bias_proj, bias_fc1, bias_fc2, grad_cond), ("dp", "seq")
    )
    loss = summed[0] / divisor
    block_out = jnp.stack(results, axis=0)
    latents_grad = jnp.stack(input_grads, axis=0)
    return (
        block_out,
        latents_grad,
        loss,
        summed[6],
        ada_w_grad,
        summed[1],
        qkv_w_grad,
        summed[2],
        proj_w_grad,
        summed[3],
        fc1_w_grad,
        summed[4],
        fc2_w_grad,
        summed[5],
    )


def solution(mesh):
    placed = (
        P(None, "dp", "seq", None),
        P(),
        P(),
        P(),
        P(None, "dp", "seq", None),
        P(None, "dp", "seq", None),
        P("dp", "seq"),
        P(),
        P("dp", "seq"),
        P(),
        P("dp", "seq"),
        P(),
        P("dp", "seq"),
        P(),
        P("dp", "seq"),
        P(),
    )
    return jax.shard_map(
        local,
        mesh=mesh,
        in_specs=placed,
        out_specs=(
            P(None, "dp", "seq", None),
            P(None, "dp", "seq", None),
            P(),
            P(),
            P("dp", "seq"),
            P(),
            P("dp", "seq"),
            P(),
            P("dp", "seq"),
            P(),
            P("dp", "seq"),
            P(),
            P("dp", "seq"),
            P(),
        ),
        check_vma=False,
    )
```

profile of v0, /device:TPU:8, one launch (start us, length us, event | category | flops | bytes accessed | tf_op | source)
XLA Modules:
  0.0 1624.2 jit_solution(10174713782407896748)
XLA Ops:
  7.3 16.6 %all_gather.52 = bf16[72,6912]{1,0:T(8,128)(2,1)} all-gather(bf16[72,3456]{1,0:T(8,128)(2,1)} %param.22), channel_id=1, replica_groups=mesh['dp'=16,'seq'=2] {'seq'}, dimensions={1}, use_global_device_ids=true | all-gather | bytes 1492992 | tf_op jit(solution)/shard_map/all_gather | solution.py:82
  40.4 103.6 %all-gather.13.cloned.1.call-done = bf16[1152,6912]{1,0:T(8,128)(2,1)} async-done(((bf16[72,6912]{1,0:T(8,128)(2,1)}), bf16[1152,6912]{1,0:T(8,128)(2,1)}) %all-gather.13.cloned.1.call-update) | async-done | bytes 15925264 | tf_op jit(solution)/shard_map/all_gather | solution.py:83
  156.9 61.6 %all-gather.15.cloned.1.call-done = bf16[1152,3456]{1,0:T(8,128)(2,1)} async-done(((bf16[72,3456]{1,0:T(8,128)(2,1)}), bf16[1152,3456]{1,0:T(8,128)(2,1)}) %all-gather.15.cloned.1.call-update) | async-done | bytes 7962640 | tf_op jit(solution)/shard_map/all_gather | solution.py:78
  256.4 17.8 %all_gather.60 = bf16[72,4608]{1,0:T(8,128)(2,1)} all-gather(bf16[72,2304]{1,0:T(8,128)(2,1)S(1)} %copy-done.31), channel_id=1, replica_groups=mesh['dp'=16,'seq'=2] {'seq'}, dimensions={1}, use_global_device_ids=true | all-gather | bytes 995328 | tf_op jit(solution)/shard_map/all_gather | solution.py:76
  297.4 15.1 all-gather.27.cloned.1.call-done
  316.8 33.2 %all-gather.17.cloned.1.call-done = bf16[1,1024,1152]{2,1,0:T(8,128)(2,1)} async-done(((bf16[1,512,1152]{2,1,0:T(8,128)(2,1)}), bf16[1,1024,1152]{2,1,0:T(8,128)(2,1)}) %all-gather.17.cloned.1.call-update) | async-done | bytes 2359312 | tf_op jit(solution)/shard_map/all_gather | solution.py:114
  354.3 33.2 %all-gather.19.cloned.1.call-done = bf16[1,1024,1152]{2,1,0:T(8,128)(2,1)} async-done(((bf16[1,512,1152]{2,1,0:T(8,128)(2,1)}), bf16[1,1024,1152]{2,1,0:T(8,128)(2,1)}) %all-gather.19.cloned.1.call-update) | async-done | bytes 2359312 | tf_op jit(solution)/shard_map/all_gather | solution.py:113
  391.8 17.5 %fusion.192 = (f32[16,512]{1,0:T(8,128)S(1)}, f32[16,512,1024]{2,1,0:T(8,128)}) fusion(bf16[512,16,72]{0,2,1:T(8,128)(2,1)} %bitcast.285, bf16[1024,16,72]{0,2,1:T(8,128)(2,1)} %bitcast.281), kind=kOutput, calls=%fused_computation.324 | convolution fusion | flops 1233126400 | bytes 37126144 | tf_op jit(solution)/shard_map/sub | solution.py:125
  409.3 15.5 fusion.97
  438.8 17.6 %fusion.191 = (f32[16,512]{1,0:T(8,128)S(1)}, f32[16,512,1024]{2,1,0:T(8,128)}) fusion(bf16[512,16,72]{0,2,1:T(8,128)(2,1)} %bitcast.287, bf16[1024,16,72]{0,2,1:T(8,128)(2,1)} %bitcast.283), kind=kOutput, calls=%fused_computation.323 | convolution fusion | flops 1233126400 | bytes 37126144 | tf_op jit(solution)/shard_map/sub | solution.py:125
  456.5 15.2 fusion.94
  481.7 40.6 %all-gather.23.cloned.1.call-done = bf16[1152,4608]{1,0:T(8,128)(2,1)} async-done(((bf16[72,4608]{1,0:T(8,128)(2,1)}), bf16[1152,4608]{1,0:T(8,128)(2,1)}) %all-gather.23.cloned.1.call-update) | async-done | bytes 10616848 | tf_op jit(solution)/shard_map/all_gather | solution.py:80
  544.2 67.8 %all-gather.25.cloned.1.call-done = bf16[4608,1152]{1,0:T(8,128)(2,1)} async-done(((bf16[288,1152]{1,0:T(8,128)(2,1)}), bf16[4608,1152]{1,0:T(8,128)(2,1)}) %all-gather.25.cloned.1.call-update) | async-done | bytes 10616848 | tf_op jit(solution)/shard_map/all_gather | solution.py:81
  625.9 20.5 %convert_reduce_fusion.5 = (f32[1152]{0:T(1024)}, bf16[512,1152]{1,0:T(8,128)(2,1)}, f32[512,1152]{1,0:T(8,128)}, f32[512,1152]{1,0:T(8,128)}, f32[1152]{0:T(102...) fusion(f32[1152]{0:T(1024)S(1)} %copy-done.92, ...), kind=kOutput, calls=%fused_computation.144 | convolution fusion | flops 5475334144 | bytes 46047756 | tf_op jit(solution)/shard_map/btf,fd->btd/dot_general | solution.py:134
  659.7 25.6 %convert_reduce_fusion.1 = (f32[4608]{0:T(1024)}, bf16[512,4608]{1,0:T(8,128)(2,1)}, f32[4608]{0:T(1024)}, bf16[512,4608]{1,0:T(8,128)(2,1)S(1)}) fusion(f32[512,4608]{1,0:T(8,128)} %fusion.171, f32[4608]{0:T(1024)S(1)} %copy-done.100, f32[512,4608]{1,0:T(8,128)} %fusion.194, f32[512,4608]{1,0:T(8,128)} %fusion.172, bf16[512,1152]{1,0:T(8,128)(2,1)S(1)} %copy-done.106, ...), kind=kOutput, calls=%fused_computation.43 | convolution fusion | flops 5544336384 | bytes 49600512 | tf_op jit(solution)/shard_map/btd,fd->btf/dot_general | solution.py:145
  742.2 23.2 %multiply_reduce_fusion.1 = (f32[16,512]{1,0:T(8,128)S(1)}, f32[16,512,1024]{2,1,0:T(8,128)}) fusion(f32[16,512,1024]{2,1,0:T(8,128)} %get-tuple-element.114, f32[16,512]{1,0:T(8,128)S(1)} %copy-done.46, bf16[512,16,72]{0,2,1:T(8,128)(2,1)} %bitcast.312, bf16[1024,16,72]{0,2,1:T(8,128)(2,1)} %bitcast.301), kind=kOutput, calls=%fused_computation.5 | convolution fusion | flops 1233117184 | bytes 70713344 | tf_op jit(solution)/shard_map/bqhe,bkhe->bhqk/dot_general | solution.py:170
  785.0 28.2 %multiply_convert_fusion.1 = bf16[16,512,1024]{2,1,0:T(8,128)(2,1)} fusion(f32[16,512,1024]{2,1,0:T(8,128)} %get-tuple-element.121, f32[16,512]{1,0:T(8,128)S(1)} %get-tuple-element.120, f32[16,512,1024]{2,1,0:T(8,128)} %get-tuple-element.114, f32[16,512]{1,0:T(8,128)S(1)} %copy-done.46), kind=kLoop, calls=%fused_computation.4 | loop fusion | flops 33554432 | bytes 83951616 | tf_op jit(solution)/shard_map/convert_element_type | solution.py:172
  824.4 14.6 fusion.91
  839.0 22.9 %multiply_reduce_fusion = (f32[16,512]{1,0:T(8,128)S(1)}, f32[16,512,1024]{2,1,0:T(8,128)}) fusion(f32[16,512,1024]{2,1,0:T(8,128)} %get-tuple-element.116, f32[16,512]{1,0:T(8,128)S(1)} %copy-done.44, bf16[512,16,72]{0,2,1:T(8,128)(2,1)} %bitcast.311, bf16[1024,16,72]{0,2,1:T(8,128)(2,1)S(1)} %bitcast.299), kind=kOutput, calls=%fused_computation.3 | convolution fusion | flops 1233117184 | bytes 70713344 | tf_op jit(solution)/shard_map/bqhe,bkhe->bhqk/dot_general | solution.py:170
  862.0 28.2 %multiply_convert_fusion = bf16[16,512,1024]{2,1,0:T(8,128)(2,1)} fusion(f32[16,512,1024]{2,1,0:T(8,128)} %get-tuple-element.126, f32[16,512]{1,0:T(8,128)S(1)} %get-tuple-element.125, f32[16,512,1024]{2,1,0:T(8,128)} %get-tuple-element.116, f32[16,512]{1,0:T(8,128)S(1)} %copy-done.44), kind=kLoop, calls=%fused_computation.2 | loop fusion | flops 33554432 | bytes 83951616 | tf_op jit(solution)/shard_map/convert_element_type | solution.py:172
  916.2 17.1 %fusion.9 = bf16[4608,1152]{1,0:T(8,128)(2,1)} fusion(f32[4608,1152]{1,0:T(8,128)} %fusion.173, bf16[512,1152]{1,0:T(8,128)(2,1)S(1)} %copy-done.105, f32[512,4608]{1,0:T(8,128)} %fusion.172, f32[4608]{0:T(1024)S(1)} %copy-done.101), kind=kOutput, calls=%fused_computation.15 | convolution fusion | flops 5470027776 | bytes 42485760 | tf_op jit(solution)/shard_map/btf,btd->fd/dot_general | solution.py:143
  947.0 16.2 fusion.8
  1007.2 14.9 fusion.12
  1048.1 16.8 %all-reduce.4 = (bf16[1,6912]{1,0:T(2,128)(2,1)S(1)}, bf16[1,6912]{1,0:T(2,128)(2,1)S(1)}) all-reduce(f32[1,6912]{1,0:T(1,128)S(1)} %constant_dynamic-update-slice_fusion.6, f32[1,6912]{1,0:T(1,128)S(1)} %constant_dynamic-update-slice_fusion), channel_id=1, replica_groups=mesh['dp'=16,'seq'=2] {'seq'}, use_global_device_ids=true, to_apply=%region_43.44 | all-reduce | flops 13824 | bytes 82944 | tf_op jit(solution)/shard_map/psum | solution.py:209
  1079.1 122.1 %reduce-scatter.34.cloned.1.call-done = bf16[72,4608]{1,0:T(8,128)(2,1)} async-done(((bf16[1152,4608]{1,0:T(8,128)(2,1)}), bf16[72,4608]{1,0:T(8,128)(2,1)}) %reduce-scatter.34.cloned.1.call-update) | async-done | bytes 663568 | tf_op jit(solution)/shard_map/reduce_scatter | solution.py:227
  1223.0 98.0 %reduce-scatter.48.cloned.1.call-done = bf16[72,3456]{1,0:T(8,128)(2,1)} async-done(((bf16[1152,3456]{1,0:T(8,128)(2,1)}), bf16[72,3456]{1,0:T(8,128)(2,1)}) %reduce-scatter.48.cloned.1.call-update) | async-done | bytes 497680
  1337.6 45.3 %all-reduce.3 = (f32[]{:T(128)}, f32[6912]{0:T(1024)}, f32[2304]{0:T(1024)}, f32[1152]{0:T(1024)}, f32[4608]{0:T(1024)}, /*index=5*/f32[1152]{0:T(1024)}) all-reduce(f32[]{:T(128)S(6)} %add.469, f32[6912]{0:T(1024)S(1)} %select_add_fusion, f32[2304]{0:T(1024)S(1)} %maximum_add_fusion, ...), channel_id=1, replica_groups=mesh['dp'=16,'seq'=2] {'dp','seq'}, use_global_device_ids=true, to_apply=%region_29.30 | all-reduce | flops 16129 | bytes 129032 | tf_op jit(solution)/shard_map/psum | solution.py:248
  1383.6 42.7 %reduce-scatter.46.cloned.1.call-done = bf16[72,3456]{1,0:T(8,128)(2,1)} async-done(((bf16[1152,3456]{1,0:T(8,128)(2,1)}), bf16[72,3456]{1,0:T(8,128)(2,1)}) %reduce-scatter.46.cloned.1.call-update) | async-done | bytes 497680
  1428.4 18.5 %reduce-scatter.44.cloned.1.call-done = bf16[576,288]{1,0:T(8,128)(2,1)} async-done(((bf16[1152,288]{1,0:T(8,128)(2,1)}), bf16[576,288]{1,0:T(8,128)(2,1)}) %reduce-scatter.44.cloned.1.call-update) | async-done | bytes 331792
  1449.0 16.3 %reduce-scatter.36.cloned.1.call-done = bf16[72,2304]{1,0:T(8,128)(2,1)} async-done(((bf16[72,4608]{1,0:T(8,128)(2,1)}), bf16[72,2304]{1,0:T(8,128)(2,1)}) %reduce-scatter.36.cloned.1.call-update) | async-done | bytes 331792 | tf_op jit(solution)/shard_map/reduce_scatter | solution.py:241
  1467.1 19.0 %reduce-scatter.40.cloned.1.call-done = bf16[1728,72]{1,0:T(8,128)(2,1)} async-done(((bf16[3456,72]{1,0:T(8,128)(2,1)}), bf16[1728,72]{1,0:T(8,128)(2,1)}) %reduce-scatter.40.cloned.1.call-update) | async-done | bytes 248848
  1488.1 126.6 %all-reduce.7.cloned.1.call-done = f32[24,1152]{1,0:T(8,128)} async-done(((f32[24,1152]{1,0:T(8,128)}), f32[24,1152]{1,0:T(8,128)}) %all-reduce.7.cloned.1.call-update) | async-done | bytes 110608 | tf_op jit(solution)/shard_map/psum | solution.py:248
  (414 shorter events, 432.7 us)
Async XLA Ops:
  7.2 136.8 %all-gather.13.cloned.1.call-start = ((), (), s32[]{:S(2)}) async-start(), calls=%async_computation.13 | async-start | bytes 16920576 | tf_op jit(solution)/shard_map/all_gather | solution.py:83
  23.9 194.6 %all-gather.15.cloned.1.call-start = ((), (), s32[]{:S(2)}) async-start(), calls=%async_computation.14 | async-start | bytes 8460288 | tf_op jit(solution)/shard_map/all_gather | solution.py:78
  33.8 259.4 %all-gather.29.cloned.1.call-start = ((), (), s32[]{:S(2)}) async-start(), calls=%async_computation.21 | async-start | bytes 3538944 | tf_op jit(solution)/shard_map/all_gather | solution.py:113
  39.0 192.0 %copy-start.69 = (f32[512]{0:T(512)}, f32[512]{0:T(512)S(1)}, u32[]{:S(2)}) copy-start(f32[512]{0:T(512)S(1)} %get-tuple-element.137) | copy-start | bytes 6148
  156.9 378.2 %copy-start.87 = (f32[1152]{0:T(1024)}, f32[1152]{0:T(1024)S(1)}, u32[]{:S(2)}) copy-start(f32[1152]{0:T(1024)S(1)} %get-tuple-element.40) | copy-start | bytes 13828
  156.9 555.9 %copy-start.50 = (f32[1152]{0:T(1024)}, f32[1152]{0:T(1024)S(1)}, u32[]{:S(2)}) copy-start(f32[1152]{0:T(1024)S(1)} %get-tuple-element.41) | copy-start | bytes 13828
  230.4 82.2 %all-gather.27.cloned.1.call-start = ((), (), s32[]{:S(2)}) async-start(), calls=%async_computation.20 | async-start | bytes 3538944 | tf_op jit(solution)/shard_map/all_gather | solution.py:114
  231.0 291.2 %copy-start.89 = (f32[1152]{0:T(1024)}, f32[1152]{0:T(1024)S(1)}, u32[]{:S(2)}) copy-start(f32[1152]{0:T(1024)S(1)} %get-tuple-element.34) | copy-start | bytes 13828
  231.0 481.1 %copy-start.53 = (f32[1152]{0:T(1024)}, f32[1152]{0:T(1024)S(1)}, u32[]{:S(2)}) copy-start(f32[1152]{0:T(1024)S(1)} %get-tuple-element.35) | copy-start | bytes 13828
  243.4 106.6 %all-gather.17.cloned.1.call-start = ((), (), s32[]{:S(2)}) async-start(), calls=%async_computation.15 | async-start | bytes 3538944 | tf_op jit(solution)/shard_map/all_gather | solution.py:114
  244.0 143.5 %all-gather.19.cloned.1.call-start = ((), (), s32[]{:S(2)}) async-start(), calls=%async_computation.16 | async-start | bytes 3538944 | tf_op jit(solution)/shard_map/all_gather | solution.py:113
  246.9 186.5 %all-gather.21.cloned.1.call-start = ((), (), s32[]{:S(2)}) async-start(), calls=%async_computation.17 | async-start | bytes 2820096 | tf_op jit(solution)/shard_map/all_gather | solution.py:79
  256.4 265.9 %all-gather.23.cloned.1.call-start = ((), (), s32[]{:S(2)}) async-start(), calls=%async_computation.18 | async-start | bytes 11280384 | tf_op jit(solution)/shard_map/all_gather | solution.py:80
  274.3 337.7 %all-gather.25.cloned.1.call-start = ((), (), s32[]{:S(2)}) async-start(), calls=%async_computation.19 | async-start | bytes 11280384 | tf_op jit(solution)/shard_map/all_gather | solution.py:81
  286.3 706.0 %reduce-scatter.50.cloned.1.call-start = ((), (), s32[]{:S(2)}) async-start(), calls=%async_computation.35 | async-start | bytes 2820096
  479.5 233.4 %copy-start.65 = (f32[512]{0:T(512)}, f32[512]{0:T(512)S(1)}, u32[]{:S(2)}) copy-start(f32[512]{0:T(512)S(1)} %broadcast_multiply_fusion) | copy-start | bytes 6148
  479.8 232.3 %copy-start.67 = (f32[512]{0:T(512)}, f32[512]{0:T(512)S(1)}, u32[]{:S(2)}) copy-start(f32[512]{0:T(512)S(1)} %broadcast_multiply_fusion.2) | copy-start | bytes 6148
  481.6 231.2 %copy-start.77 = (f32[512]{0:T(512)}, f32[512]{0:T(512)S(1)}, u32[]{:S(2)}) copy-start(f32[512]{0:T(512)S(1)} %fusion.155) | copy-start | bytes 6148
  481.6 230.5 %copy-start.79 = (f32[512]{0:T(512)}, f32[512]{0:T(512)S(1)}, u32[]{:S(2)}) copy-start(f32[512]{0:T(512)S(1)} %fusion.153) | copy-start | bytes 6148
  741.5 253.1 %reduce-scatter.28.cloned.1.call-start = ((), (), s32[]{:S(2)}) async-start(), calls=%async_computation.23 | async-start | bytes 3538944 | tf_op jit(solution)/shard_map/reduce_scatter | solution.py:188
  785.0 209.7 %reduce-scatter.26.cloned.1.call-start = ((), (), s32[]{:S(2)}) async-start(), calls=%async_computation.22 | async-start | bytes 3538944 | tf_op jit(solution)/shard_map/reduce_scatter | solution.py:185
  823.6 183.5 %reduce-scatter.32.cloned.1.call-start = ((), (), s32[]{:S(2)}) async-start(), calls=%async_computation.25 | async-start | bytes 3538944 | tf_op jit(solution)/shard_map/reduce_scatter | solution.py:188
  862.0 145.2 %reduce-scatter.30.cloned.1.call-start = ((), (), s32[]{:S(2)}) async-start(), calls=%async_computation.24 | async-start | bytes 3538944 | tf_op jit(solution)/shard_map/reduce_scatter | solution.py:185
  900.6 176.1 %reduce-scatter.38.cloned.1.call-start = ((), (), s32[]{:S(2)}) async-start(), calls=%async_computation.29 | async-start | bytes 11280384 | tf_op jit(solution)/shard_map/reduce_scatter | solution.py:230
  933.5 267.7 %reduce-scatter.34.cloned.1.call-start = ((), (), s32[]{:S(2)}) async-start(), calls=%async_computation.27 | async-start | bytes 11280384 | tf_op jit(solution)/shard_map/reduce_scatter | solution.py:227
  963.2 252.5 %reduce-scatter.42.cloned.1.call-start = ((), (), s32[]{:S(2)}) async-start(), calls=%async_computation.31 | async-start | bytes 442368
  994.1 326.9 %reduce-scatter.48.cloned.1.call-start = ((), (), s32[]{:S(2)}) async-start(), calls=%async_computation.34 | async-start | bytes 8460288
  1022.1 404.2 %reduce-scatter.46.cloned.1.call-start = ((), (), s32[]{:S(2)}) async-start(), calls=%async_computation.33 | async-start | bytes 8460288
  1071.2 375.6 %reduce-scatter.44.cloned.1.call-start = ((), (), s32[]{:S(2)}) async-start(), calls=%async_computation.32 | async-start | bytes 1327104
  1079.0 386.2 %reduce-scatter.36.cloned.1.call-start = ((), (), s32[]{:S(2)}) async-start(), calls=%async_computation.28 | async-start | bytes 995328 | tf_op jit(solution)/shard_map/reduce_scatter | solution.py:241
  1201.2 284.9 %reduce-scatter.40.cloned.1.call-start = ((), (), s32[]{:S(2)}) async-start(), calls=%async_computation.30 | async-start | bytes 1327104
  1323.4 291.3 %all-reduce.7.cloned.1.call-start = ((), (), s32[]{:S(2)}) async-start(), calls=%async_computation.26 | async-start | bytes 221184 | tf_op jit(solution)/shard_map/psum | solution.py:248
  (101 other events, 2285.7 us)
Sparse Core Ops, SparseCore 0:
  24.0 119.9 all-gather.12
  146.7 71.7 all-gather.14
  230.5 43.9 all-gather.28
  276.4 36.0 all-gather.26
  313.9 36.0 all-gather.16
  351.4 36.0 all-gather.18
  390.2 43.1 all-gather.20
  435.7 86.4 all-gather.22
  525.1 86.8 all-gather.24
  741.6 62.4 reduce-scatter.49
  806.4 34.1 reduce-scatter.27
  842.7 34.7 reduce-scatter.25
  879.8 34.6 reduce-scatter.31
  917.2 34.7 reduce-scatter.29
  956.4 120.2 reduce-scatter.37
  1081.1 119.9 reduce-scatter.33
  1203.9 11.7 reduce-scatter.41
  1220.2 100.8 reduce-scatter.47
  1325.1 101.1 reduce-scatter.45
  1428.5 18.2 reduce-scatter.43
  1449.2 16.0 reduce-scatter.35
  1467.5 18.5 reduce-scatter.39
  1492.3 122.4 all-reduce.6
where the time goes:
time: 1630 us; the launch traced here: 1620 us
  waiting for transfers between devices  816 us (50%)
  matrix products  485 us (30%)
  blocking collectives  123 us (8%)
  other arithmetic  113 us (7%)
  local copies, waits for them, and re-layouts  66.1 us (4%)
  between operations  19.4 us (1%)
    unnamed x29, waiting for transfers between devices  182 us
    psum x1, waiting for transfers between devices, local(): lax.psum((loss_sum, bias_ada, bias_qv, bias_proj, bias_fc1, bias_fc2, gra...  127 us
    reduce_scatter x1, waiting for transfers between devices, local(): lax.psum_scatter(grad_fc1.astype(jnp.bfloat16), 'dp', scatter_dimension=0...  122 us
    all_gather x1, waiting for transfers between devices, local(): ada_full = lax.all_gather(ada_cols, 'dp', axis=0, tiled=True)  104 us
    all_gather x1, waiting for transfers between devices, local(): fc2_full = lax.all_gather(fc2_cols, 'dp', axis=0, tiled=True)  67.8 us
    all_gather x1, waiting for transfers between devices, local(): qkv_full = lax.all_gather(qkv_cols, 'dp', axis=0, tiled=True)  61.6 us
    convert_element_type x2, other arithmetic, local(): d_scores = (probs * (d_probs - row_inner)).astype(bf16)  56.5 us
    all_gather x2, waiting for transfers between devices, local(): lax.all_gather(values_local, 'seq', axis=1, tiled=True)  48.3 us
  transfers between devices with their start and end apart: 23, of which 17 were waited for; matrix products, arithmetic and copies ran while one was open for 31% of the time, Pallas kernels for 0%

commit v1 on v0

--- a/solution.py
+++ b/solution.py
@@ -246,7 +246,8 @@
         ).astype(jnp.float32),
     )
     summed = lax.psum(
-        (loss_sum, bias_ada, bias_qv, bias_proj, bias_fc1, bias_fc2, grad_cond), ("dp", "seq")
+        lax.psum((loss_sum, bias_ada, bias_qv, bias_proj, bias_fc1, bias_fc2, grad_cond), "dp"),
+        "seq",
     )
     loss = summed[0] / divisor
     block_out = jnp.stack(results, axis=0)

time: 1630 us -> 1660 us (1.018)
    psum x1, waiting for transfers between devices: 127 us -> 87.4 us  [local(): lax.psum((loss_sum, bias_ada, bias_qv, bias_proj, bias_fc1, bias_fc2, gra...]
    reduce_scatter x1, waiting for transfers between devices: 5.22 us -> 35.6 us  [local(): lax.psum_scatter(grad_fc2.astype(jnp.bfloat16), 'dp', scatter_dimension=0...]
    psum x0 -> x1, waiting for transfers between devices: none -> 21.3 us  [local(): lax.psum(lax.psum((loss_sum, bias_ada, bias_qv, bias_proj, bias_fc1, bias...]
    unnamed x29 -> x30, waiting for transfers between devices: 182 us -> 182 us
    unnamed x240 -> x246, local copies, waits for them, and re-layouts: 33.1 us -> 33.2 us
  transfers between devices with their start and end apart: 23 -> 24, of which waited for: 17 -> 18; matrix products, arithmetic and copies ran while one was open for 31% -> 29% of each run, Pallas kernels for 0% -> 0%
where the time goes in v1:
time: 1660 us; the launch traced here: 1650 us
  waiting for transfers between devices  829 us (50%)
  matrix products  480 us (29%)
  blocking collectives  139 us (8%)
  other arithmetic  110 us (7%)
  local copies, waits for them, and re-layouts  66.1 us (4%)
  between operations  19.9 us (1%)
    unnamed x30, waiting for transfers between devices  182 us
    reduce_scatter x1, waiting for transfers between devices, local(): lax.psum_scatter(grad_fc1.astype(jnp.bfloat16), 'dp', scatter_dimension=0...  122 us
    all_gather x1, waiting for transfers between devices, local(): ada_full = lax.all_gather(ada_cols, 'dp', axis=0, tiled=True)  104 us
    psum x1, waiting for transfers between devices, local(): lax.psum((loss_sum, bias_ada, bias_qv, bias_proj, bias_fc1, bias_fc2, gra...  87.4 us
    all_gather x1, waiting for transfers between devices, local(): fc2_full = lax.all_gather(fc2_cols, 'dp', axis=0, tiled=True)  68.1 us
    all_gather x1, waiting for transfers between devices, local(): qkv_full = lax.all_gather(qkv_cols, 'dp', axis=0, tiled=True)  61.6 us
    convert_element_type x2, other arithmetic, local(): d_scores = (probs * (d_probs - row_inner)).astype(bf16)  56.7 us
    psum x1, blocking collectives, local(): lax.psum((loss_sum, bias_ada, bias_qv, bias_proj, bias_fc1, bias_fc2, gra...  52 us
  transfers between devices with their start and end apart: 24, of which 18 were waited for; matrix products, arithmetic and copies ran while one was open for 29% of the time, Pallas kernels for 0%

profile of v1, /device:TPU:8, one launch (start us, length us, event | category | flops | bytes accessed | tf_op | source)
XLA Modules:
  0.0 1645.5 jit_solution(5444971359637359001)
XLA Ops:
  7.3 16.6 %all_gather.52 = bf16[72,6912]{1,0:T(8,128)(2,1)} all-gather(bf16[72,3456]{1,0:T(8,128)(2,1)} %param.22), channel_id=1, replica_groups=mesh['dp'=16,'seq'=2] {'seq'}, dimensions={1}, use_global_device_ids=true | all-gather | bytes 1492992 | tf_op jit(solution)/shard_map/all_gather | solution.py:82
  40.2 103.7 %all-gather.13.cloned.1.call-done = bf16[1152,6912]{1,0:T(8,128)(2,1)} async-done(((bf16[72,6912]{1,0:T(8,128)(2,1)}), bf16[1152,6912]{1,0:T(8,128)(2,1)}) %all-gather.13.cloned.1.call-update) | async-done | bytes 15925264 | tf_op jit(solution)/shard_map/all_gather | solution.py:83
  156.9 61.6 %all-gather.15.cloned.1.call-done = bf16[1152,3456]{1,0:T(8,128)(2,1)} async-done(((bf16[72,3456]{1,0:T(8,128)(2,1)}), bf16[1152,3456]{1,0:T(8,128)(2,1)}) %all-gather.15.cloned.1.call-update) | async-done | bytes 7962640 | tf_op jit(solution)/shard_map/all_gather | solution.py:78
  256.4 17.9 %all_gather.60 = bf16[72,4608]{1,0:T(8,128)(2,1)} all-gather(bf16[72,2304]{1,0:T(8,128)(2,1)S(1)} %copy-done.32), channel_id=1, replica_groups=mesh['dp'=16,'seq'=2] {'seq'}, dimensions={1}, use_global_device_ids=true | all-gather | bytes 995328 | tf_op jit(solution)/shard_map/all_gather | solution.py:76
  316.8 33.2 %all-gather.17.cloned.1.call-done = bf16[1,1024,1152]{2,1,0:T(8,128)(2,1)} async-done(((bf16[1,512,1152]{2,1,0:T(8,128)(2,1)}), bf16[1,1024,1152]{2,1,0:T(8,128)(2,1)}) %all-gather.17.cloned.1.call-update) | async-done | bytes 2359312 | tf_op jit(solution)/shard_map/all_gather | solution.py:114
  354.3 33.2 %all-gather.19.cloned.1.call-done = bf16[1,1024,1152]{2,1,0:T(8,128)(2,1)} async-done(((bf16[1,512,1152]{2,1,0:T(8,128)(2,1)}), bf16[1,1024,1152]{2,1,0:T(8,128)(2,1)}) %all-gather.19.cloned.1.call-update) | async-done | bytes 2359312 | tf_op jit(solution)/shard_map/all_gather | solution.py:113
  391.8 17.5 %fusion.192 = (f32[16,512]{1,0:T(8,128)S(1)}, f32[16,512,1024]{2,1,0:T(8,128)}) fusion(bf16[512,16,72]{0,2,1:T(8,128)(2,1)} %bitcast.285, bf16[1024,16,72]{0,2,1:T(8,128)(2,1)} %bitcast.281), kind=kOutput, calls=%fused_computation.324 | convolution fusion | flops 1233126400 | bytes 37126144 | tf_op jit(solution)/shard_map/sub | solution.py:125
  409.3 15.5 fusion.97
  438.9 17.7 %fusion.191 = (f32[16,512]{1,0:T(8,128)S(1)}, f32[16,512,1024]{2,1,0:T(8,128)}) fusion(bf16[512,16,72]{0,2,1:T(8,128)(2,1)} %bitcast.287, bf16[1024,16,72]{0,2,1:T(8,128)(2,1)} %bitcast.283), kind=kOutput, calls=%fused_computation.323 | convolution fusion | flops 1233126400 | bytes 37126144 | tf_op jit(solution)/shard_map/sub | solution.py:125
  481.5 40.7 %all-gather.23.cloned.1.call-done = bf16[1152,4608]{1,0:T(8,128)(2,1)} async-done(((bf16[72,4608]{1,0:T(8,128)(2,1)}), bf16[1152,4608]{1,0:T(8,128)(2,1)}) %all-gather.23.cloned.1.call-update) | async-done | bytes 10616848 | tf_op jit(solution)/shard_map/all_gather | solution.py:80
  544.0 68.1 %all-gather.25.cloned.1.call-done = bf16[4608,1152]{1,0:T(8,128)(2,1)} async-done(((bf16[288,1152]{1,0:T(8,128)(2,1)}), bf16[4608,1152]{1,0:T(8,128)(2,1)}) %all-gather.25.cloned.1.call-update) | async-done | bytes 10616848 | tf_op jit(solution)/shard_map/all_gather | solution.py:81
  625.9 21.0 %convert_reduce_fusion.5 = (f32[1152]{0:T(1024)}, bf16[512,1152]{1,0:T(8,128)(2,1)}, f32[512,1152]{1,0:T(8,128)}, f32[512,1152]{1,0:T(8,128)}, f32[1152]{0:T(102...) fusion(f32[1152]{0:T(1024)S(1)} %copy-done.98, ...), kind=kOutput, calls=%fused_computation.144 | convolution fusion | flops 5475334144 | bytes 46047756 | tf_op jit(solution)/shard_map/btf,fd->btd/dot_general | solution.py:134
  656.3 26.3 %convert_reduce_fusion.1 = (f32[4608]{0:T(1024)}, bf16[512,4608]{1,0:T(8,128)(2,1)}, f32[4608]{0:T(1024)}, bf16[512,4608]{1,0:T(8,128)(2,1)}) fusion(f32[512,4608]{1,0:T(8,128)} %fusion.171, f32[4608]{0:T(1024)S(1)} %copy-done.106, f32[512,4608]{1,0:T(8,128)S(1)} %fusion.194, f32[512,4608]{1,0:T(8,128)} %fusion.172, ...), kind=kOutput, calls=%fused_computation.43 | convolution fusion | flops 5544336384 | bytes 49600512 | tf_op jit(solution)/shard_map/btd,fd->btf/dot_general | solution.py:145
  720.8 23.2 %multiply_reduce_fusion.1 = (f32[16,512]{1,0:T(8,128)S(1)}, f32[16,512,1024]{2,1,0:T(8,128)}) fusion(f32[16,512,1024]{2,1,0:T(8,128)} %get-tuple-element.120, f32[16,512]{1,0:T(8,128)S(1)} %get-tuple-element.119, bf16[512,16,72]{0,2,1:T(8,128)(2,1)} %bitcast.313, bf16[1024,16,72]{0,2,1:T(8,128)(2,1)} %bitcast.303), kind=kOutput, calls=%fused_computation.5 | convolution fusion | flops 1233117184 | bytes 70713344 | tf_op jit(solution)/shard_map/bqhe,bkhe->bhqk/dot_general | solution.py:170
  769.5 28.2 %multiply_convert_fusion.1 = bf16[16,512,1024]{2,1,0:T(8,128)(2,1)} fusion(f32[16,512,1024]{2,1,0:T(8,128)} %get-tuple-element.127, f32[16,512]{1,0:T(8,128)S(1)} %get-tuple-element.126, f32[16,512,1024]{2,1,0:T(8,128)} %get-tuple-element.120, f32[16,512]{1,0:T(8,128)S(1)} %get-tuple-element.119), kind=kLoop, calls=%fused_computation.4 | loop fusion | flops 33554432 | bytes 83951616 | tf_op jit(solution)/shard_map/convert_element_type | solution.py:172
  808.7 15.2 fusion.91
  823.9 22.8 %multiply_reduce_fusion = (f32[16,512]{1,0:T(8,128)S(1)}, f32[16,512,1024]{2,1,0:T(8,128)}) fusion(f32[16,512,1024]{2,1,0:T(8,128)} %get-tuple-element.122, f32[16,512]{1,0:T(8,128)S(1)} %copy-done.47, bf16[512,16,72]{0,2,1:T(8,128)(2,1)} %bitcast.311, bf16[1024,16,72]{0,2,1:T(8,128)(2,1)S(1)} %bitcast.299), kind=kOutput, calls=%fused_computation.3 | convolution fusion | flops 1233117184 | bytes 70713344 | tf_op jit(solution)/shard_map/bqhe,bkhe->bhqk/dot_general | solution.py:170
  846.8 28.5 %multiply_convert_fusion = bf16[16,512,1024]{2,1,0:T(8,128)(2,1)} fusion(f32[16,512,1024]{2,1,0:T(8,128)} %get-tuple-element.132, f32[16,512]{1,0:T(8,128)S(1)} %get-tuple-element.131, f32[16,512,1024]{2,1,0:T(8,128)} %get-tuple-element.122, f32[16,512]{1,0:T(8,128)S(1)} %copy-done.47), kind=kLoop, calls=%fused_computation.2 | loop fusion | flops 33554432 | bytes 83951616 | tf_op jit(solution)/shard_map/convert_element_type | solution.py:172
  908.6 16.4 fusion.9
  938.9 16.5 %fusion.8 = bf16[1152,4608]{1,0:T(8,128)(2,1)} fusion(f32[1152,4608]{1,0:T(8,128)} %fusion.170, bf16[512,4608]{1,0:T(8,128)(2,1)} %get-tuple-element.110, f32[512,1152]{1,0:T(8,128)S(1)} %copy-done.9, f32[1152]{0:T(1024)S(1)} %copy-done.94, f32[1152]{0:T(1024)S(1)} %copy-done.54, f32[512]{0:T(512)S(1)} %copy-done.84, f32[512]{0:T(512)S(1)} %copy-done.69), kind=kOutput, calls=%fused_computation.14 | convolution fusion | flops 5449383936 | bytes 38941696 | tf_op jit(solution)/shard_map/btd,btf->df/dot_general | solution.py:147
  995.4 17.1 %fusion.12 = bf16[1152,3456]{1,0:T(8,128)(2,1)} fusion(f32[1152,3456]{1,0:T(8,128)} %fusion.101, bf16[1,512,1152]{1,2,0:T(8,128)(2,1)} %reduce-scatter.32.cloned.1.call-done, bf16[1,512,1152]{1,2,0:T(8,128)(2,1)} %reduce-scatter.30.cloned.1.call-done, bf16[1,512,1152]{1,2,0:T(8,128)(2,1)} %bitcast.305, f32[1152]{0:T(1024)S(1)} %copy-done.90, ...), kind=kOutput, calls=%fused_computation.22 | convolution fusion | flops 4098981888 | bytes 28626944 | tf_op jit(solution)/shard_map/btd,bte->de/dot_general | solution.py:194
  1041.5 16.2 all-reduce.5
  1076.2 35.6 %reduce-scatter.38.cloned.1.call-done = bf16[288,1152]{1,0:T(8,128)(2,1)} async-done(((bf16[4608,1152]{1,0:T(8,128)(2,1)}), bf16[288,1152]{1,0:T(8,128)(2,1)}) %reduce-scatter.38.cloned.1.call-update) | async-done | bytes 663568 | tf_op jit(solution)/shard_map/reduce_scatter | solution.py:230
  1114.1 122.0 %reduce-scatter.34.cloned.1.call-done = bf16[72,4608]{1,0:T(8,128)(2,1)} async-done(((bf16[1152,4608]{1,0:T(8,128)(2,1)}), bf16[72,4608]{1,0:T(8,128)(2,1)}) %reduce-scatter.34.cloned.1.call-update) | async-done | bytes 663568 | tf_op jit(solution)/shard_map/reduce_scatter | solution.py:227
  1243.5 97.7 %reduce-scatter.48.cloned.1.call-done = bf16[72,3456]{1,0:T(8,128)(2,1)} async-done(((bf16[1152,3456]{1,0:T(8,128)(2,1)}), bf16[72,3456]{1,0:T(8,128)(2,1)}) %reduce-scatter.48.cloned.1.call-update) | async-done | bytes 497680
  1360.7 87.4 %all-reduce.9.cloned.1.call-done = f32[24,1152]{1,0:T(8,128)} async-done(((f32[24,1152]{1,0:T(8,128)}), f32[24,1152]{1,0:T(8,128)}) %all-reduce.9.cloned.1.call-update) | async-done | bytes 110608 | tf_op jit(solution)/shard_map/psum | solution.py:249
  1452.6 52.0 %all-reduce.3 = (f32[]{:T(128)}, f32[6912]{0:T(1024)S(1)}, f32[2304]{0:T(1024)S(1)}, f32[1152]{0:T(1024)S(1)}, f32[4608]{0:T(1024)S(1)}, /*index=5*/f32[1152]{0:T(1024)S(1)}) all-reduce(f32[]{:T(128)S(6)} %add.483, f32[6912]{0:T(1024)S(1)} %select_add_fusion, ...), channel_id=1, replica_groups=mesh['dp'=16,'seq'=2] {'dp'}, use_global_device_ids=true, to_apply=%region_29.30 | all-reduce | flops 16129 | bytes 129032 | tf_op jit(solution)/shard_map/psum | solution.py:249
  1515.3 37.2 %reduce-scatter.46.cloned.1.call-done = bf16[72,3456]{1,0:T(8,128)(2,1)} async-done(((bf16[1152,3456]{1,0:T(8,128)(2,1)}), bf16[72,3456]{1,0:T(8,128)(2,1)}) %reduce-scatter.46.cloned.1.call-update) | async-done | bytes 497680
  1554.6 18.6 %reduce-scatter.44.cloned.1.call-done = bf16[576,288]{1,0:T(8,128)(2,1)} async-done(((bf16[1152,288]{1,0:T(8,128)(2,1)}), bf16[576,288]{1,0:T(8,128)(2,1)}) %reduce-scatter.44.cloned.1.call-update) | async-done | bytes 331792
  1575.3 16.3 reduce-scatter.36.cloned.1.call-done
  1593.5 19.0 %reduce-scatter.40.cloned.1.call-done = bf16[1728,72]{1,0:T(8,128)(2,1)} async-done(((bf16[3456,72]{1,0:T(8,128)(2,1)}), bf16[1728,72]{1,0:T(8,128)(2,1)}) %reduce-scatter.40.cloned.1.call-update) | async-done | bytes 248848
  1614.5 21.3 %all-reduce.11.cloned.1.call-done = f32[24,1152]{1,0:T(8,128)} async-done(((f32[24,1152]{1,0:T(8,128)}), f32[24,1152]{1,0:T(8,128)}) %all-reduce.11.cloned.1.call-update) | async-done | bytes 110608 | tf_op jit(solution)/shard_map/psum | solution.py:248
  (424 shorter events, 461.4 us)
Async XLA Ops:
  7.2 136.8 %all-gather.13.cloned.1.call-start = ((), (), s32[]{:S(2)}) async-start(), calls=%async_computation.13 | async-start | bytes 16920576 | tf_op jit(solution)/shard_map/all_gather | solution.py:83
  23.9 194.6 %all-gather.15.cloned.1.call-start = ((), (), s32[]{:S(2)}) async-start(), calls=%async_computation.14 | async-start | bytes 8460288 | tf_op jit(solution)/shard_map/all_gather | solution.py:78
  33.8 259.4 %all-gather.29.cloned.1.call-start = ((), (), s32[]{:S(2)}) async-start(), calls=%async_computation.21 | async-start | bytes 3538944 | tf_op jit(solution)/shard_map/all_gather | solution.py:113
  38.8 192.2 %copy-start.72 = (f32[512]{0:T(512)}, f32[512]{0:T(512)S(1)}, u32[]{:S(2)}) copy-start(f32[512]{0:T(512)S(1)} %get-tuple-element.143) | copy-start | bytes 6148
  156.9 314.7 %copy-start.35 = (f32[1152]{0:T(1024)}, f32[1152]{0:T(1024)S(1)}, u32[]{:S(2)}) copy-start(f32[1152]{0:T(1024)S(1)} %get-tuple-element.44) | copy-start | bytes 13828
  156.9 377.9 %copy-start.52 = (f32[1152]{0:T(1024)}, f32[1152]{0:T(1024)S(1)}, u32[]{:S(2)}) copy-start(f32[1152]{0:T(1024)S(1)} %get-tuple-element.41) | copy-start | bytes 13828
  156.9 377.9 %copy-start.93 = (f32[1152]{0:T(1024)}, f32[1152]{0:T(1024)S(1)}, u32[]{:S(2)}) copy-start(f32[1152]{0:T(1024)S(1)} %get-tuple-element.40) | copy-start | bytes 13828
  230.4 82.2 %all-gather.27.cloned.1.call-start = ((), (), s32[]{:S(2)}) async-start(), calls=%async_computation.20 | async-start | bytes 3538944 | tf_op jit(solution)/shard_map/all_gather | solution.py:114
  231.0 291.2 %copy-start.95 = (f32[1152]{0:T(1024)}, f32[1152]{0:T(1024)S(1)}, u32[]{:S(2)}) copy-start(f32[1152]{0:T(1024)S(1)} %get-tuple-element.34) | copy-start | bytes 13828
  231.1 464.0 %copy-start.55 = (f32[1152]{0:T(1024)}, f32[1152]{0:T(1024)S(1)}, u32[]{:S(2)}) copy-start(f32[1152]{0:T(1024)S(1)} %get-tuple-element.35) | copy-start | bytes 13828
  243.4 106.6 %all-gather.17.cloned.1.call-start = ((), (), s32[]{:S(2)}) async-start(), calls=%async_computation.15 | async-start | bytes 3538944 | tf_op jit(solution)/shard_map/all_gather | solution.py:114
  244.0 143.5 %all-gather.19.cloned.1.call-start = ((), (), s32[]{:S(2)}) async-start(), calls=%async_computation.16 | async-start | bytes 3538944 | tf_op jit(solution)/shard_map/all_gather | solution.py:113
  246.9 186.5 %all-gather.21.cloned.1.call-start = ((), (), s32[]{:S(2)}) async-start(), calls=%async_computation.17 | async-start | bytes 2820096 | tf_op jit(solution)/shard_map/all_gather | solution.py:79
  256.4 265.9 %all-gather.23.cloned.1.call-start = ((), (), s32[]{:S(2)}) async-start(), calls=%async_computation.18 | async-start | bytes 11280384 | tf_op jit(solution)/shard_map/all_gather | solution.py:80
  274.3 337.8 %all-gather.25.cloned.1.call-start = ((), (), s32[]{:S(2)}) async-start(), calls=%async_computation.19 | async-start | bytes 11280384 | tf_op jit(solution)/shard_map/all_gather | solution.py:81
  286.3 696.0 %reduce-scatter.28.cloned.1.call-start = ((), (), s32[]{:S(2)}) async-start(), calls=%async_computation.23 | async-start | bytes 3538944 | tf_op jit(solution)/shard_map/reduce_scatter | solution.py:188
  479.8 215.2 %copy-start.70 = (f32[512]{0:T(512)}, f32[512]{0:T(512)S(1)}, u32[]{:S(2)}) copy-start(f32[512]{0:T(512)S(1)} %broadcast_multiply_fusion.2) | copy-start | bytes 6148
  481.5 213.5 %copy-start.85 = (f32[512]{0:T(512)}, f32[512]{0:T(512)S(1)}, u32[]{:S(2)}) copy-start(f32[512]{0:T(512)S(1)} %fusion.153) | copy-start | bytes 6148
  769.4 212.9 %reduce-scatter.26.cloned.1.call-start = ((), (), s32[]{:S(2)}) async-start(), calls=%async_computation.22 | async-start | bytes 3538944 | tf_op jit(solution)/shard_map/reduce_scatter | solution.py:185
  808.0 187.4 %reduce-scatter.32.cloned.1.call-start = ((), (), s32[]{:S(2)}) async-start(), calls=%async_computation.25 | async-start | bytes 3538944 | tf_op jit(solution)/shard_map/reduce_scatter | solution.py:188
  846.7 148.7 %reduce-scatter.30.cloned.1.call-start = ((), (), s32[]{:S(2)}) async-start(), calls=%async_computation.24 | async-start | bytes 3538944 | tf_op jit(solution)/shard_map/reduce_scatter | solution.py:185
  885.6 128.3 %reduce-scatter.50.cloned.1.call-start = ((), (), s32[]{:S(2)}) async-start(), calls=%async_computation.36 | async-start | bytes 2820096
  892.5 219.2 %reduce-scatter.38.cloned.1.call-start = ((), (), s32[]{:S(2)}) async-start(), calls=%async_computation.30 | async-start | bytes 11280384 | tf_op jit(solution)/shard_map/reduce_scatter | solution.py:230
  925.1 311.1 %reduce-scatter.34.cloned.1.call-start = ((), (), s32[]{:S(2)}) async-start(), calls=%async_computation.28 | async-start | bytes 11280384 | tf_op jit(solution)/shard_map/reduce_scatter | solution.py:227
  955.5 385.7 %reduce-scatter.48.cloned.1.call-start = ((), (), s32[]{:S(2)}) async-start(), calls=%async_computation.35 | async-start | bytes 8460288
  1012.6 343.2 %reduce-scatter.42.cloned.1.call-start = ((), (), s32[]{:S(2)}) async-start(), calls=%async_computation.32 | async-start | bytes 442368
  1015.7 432.3 %all-reduce.9.cloned.1.call-start = ((), (), s32[]{:S(2)}) async-start(), calls=%async_computation.26 | async-start | bytes 221184 | tf_op jit(solution)/shard_map/psum | solution.py:249
  1069.8 482.7 %reduce-scatter.46.cloned.1.call-start = ((), (), s32[]{:S(2)}) async-start(), calls=%async_computation.34 | async-start | bytes 8460288
  1076.1 497.0 %reduce-scatter.44.cloned.1.call-start = ((), (), s32[]{:S(2)}) async-start(), calls=%async_computation.33 | async-start | bytes 1327104
  1114.1 477.6 %reduce-scatter.36.cloned.1.call-start = ((), (), s32[]{:S(2)}) async-start(), calls=%async_computation.29 | async-start | bytes 995328 | tf_op jit(solution)/shard_map/reduce_scatter | solution.py:241
  1236.2 376.3 %reduce-scatter.40.cloned.1.call-start = ((), (), s32[]{:S(2)}) async-start(), calls=%async_computation.31 | async-start | bytes 1327104
  1343.5 292.3 %all-reduce.11.cloned.1.call-start = ((), (), s32[]{:S(2)}) async-start(), calls=%async_computation.27 | async-start | bytes 221184 | tf_op jit(solution)/shard_map/psum | solution.py:248
  (105 other events, 2167.3 us)
Sparse Core Ops, SparseCore 0:
  24.0 119.9 all-gather.12
  146.7 71.7 all-gather.14
  230.5 43.9 all-gather.28
  276.4 36.0 all-gather.26
  313.9 36.0 all-gather.16
  351.4 36.0 all-gather.18
  390.2 43.1 all-gather.20
  435.7 86.4 all-gather.22
  525.1 86.9 all-gather.24
  769.6 33.8 reduce-scatter.27
  808.1 34.3 reduce-scatter.25
  846.8 34.3 reduce-scatter.31
  885.7 34.7 reduce-scatter.29
  924.3 63.2 reduce-scatter.49
  992.0 119.6 reduce-scatter.37
  1116.2 119.9 reduce-scatter.33
  1240.7 100.5 reduce-scatter.47
  1343.9 11.8 reduce-scatter.41
  1359.8 88.2 all-reduce.8
  1452.0 100.4 reduce-scatter.45
  1554.9 18.2 reduce-scatter.43
  1575.5 16.0 reduce-scatter.35
  1593.9 18.5 reduce-scatter.39
  1614.6 21.1 all-reduce.10
